TPU v7x, 32 devices: a whole 2x2x4 slice. The times are simulated.
32 devices in a mesh: row: 8 (over y, x, core), col: 4 (over z).
Axes of the slice: x: 2, y: 2, z: 4, core: 2. Of those that a mesh axis runs over, the one named last changes fastest.
Arguments:
- out_grad: bfloat16 [640, 8192], P('col', 'row'), may hold values from -32 to 32
- gate_act: bfloat16 [640, 29568], P('row', 'col'), may hold values from -8 to 8
- up_act: bfloat16 [640, 29568], P('row', 'col'), may hold values from -6 to 6
- gate_codes: int32 [29568, 4096], P('col', 'row'), may hold values from 0 to 255
- gate_scales: int32 [512, 29568], P('row', 'col'), may hold values from 40 to 71
- up_codes: int32 [29568, 4096], P('col', 'row'), may hold values from 0 to 255
- up_scales: int32 [512, 29568], P('row', 'col'), may hold values from 40 to 71
- down_codes: int32 [8192, 14784], P('row', 'col'), may hold values from 0 to 255
- down_scales: int32 [1848, 8192], P('col', 'row'), may hold values from 40 to 71
- tensor_scales: float32 [3], replicated, may hold values from 0.001 to 0.003
Outputs:
- grad_unit: bfloat16 [640, 8192], P('col', 'row')
- grad_amax: float32 [1], replicated
All inputs are finite; a program needn't handle non-finite values. Where the computation divides by a largest or mean magnitude, that divisor is 1e-20 or more.
Results may differ from a plain program's by a relative error of at most 0.025.
Values may be sent and summed in bfloat16 or wider, within the bound.
A program may use at most 320 MiB of HBM per device.

v0:
```python
import jax
import jax.numpy as jnp
from jax import lax
from jax.sharding import PartitionSpec as P

BLOCK = 16


def fp4_values(packed):
    low_bits = jnp.bitwise_and(packed, 15)
    high_bits = jnp.bitwise_and(jnp.right_shift(packed, 4), 15)
    codes = jnp.stack([low_bits, high_bits], axis=-1).reshape(packed.shape[0], 2 * packed.shape[1])
    magnitude = jnp.bitwise_and(codes, 7).astype(jnp.float32)
    negative = jnp.right_shift(codes, 3).astype(jnp.float32)
    level = jnp.where(
        magnitude < 4.0,
        0.5 * magnitude,
        jnp.where(magnitude < 6.0, magnitude - 2.0, 2.0 * magnitude - 8.0),
    )
    return level * (1.0 - 2.0 * negative)


def e4m3_values(scale_codes):
    exponent = jnp.right_shift(scale_codes, 3)
    mantissa = jnp.bitwise_and(scale_codes, 7)
    power = jnp.left_shift(jnp.ones_like(exponent), exponent)
    normal_part = ((8 + mantissa) * power).astype(jnp.float32) / 1024.0
    subnormal = mantissa.astype(jnp.float32) / 512.0
    return jnp.where(exponent > 0, normal_part, subnormal)


def dequantize(packed, scale_codes):
    level = fp4_values(packed)
    row_total = level.shape[0]
    col_total = level.shape[1]
    block_scale = e4m3_values(scale_codes).T
    scaled = level.reshape(row_total, block_scale.shape[1], BLOCK) * block_scale[:, :, None]
    return scaled.reshape(row_total, col_total).astype(jnp.bfloat16)


def swiglu_grads(hidden_grad, gate_rows, up_rows):
    gate_value = gate_rows.astype(jnp.float32)
    up_value = up_rows.astype(jnp.float32)
    sigmoid_gate = jax.nn.sigmoid(gate_value)
    gate_grad = (
        hidden_grad * up_value * sigmoid_gate * (1.0 + gate_value * (1.0 - sigmoid_gate))
    ).astype(jnp.bfloat16)
    up_grad = (hidden_grad * gate_value * sigmoid_gate).astype(jnp.bfloat16)
    return (gate_grad, up_grad)


def per_device(
    out_grad,
    gate_act,
    up_act,
    gate_codes,
    gate_scales,
    up_codes,
    up_scales,
    down_codes,
    down_scales,
    tensor_scales,
):
    weight_down = dequantize(down_codes, down_scales)
    weight_gate = dequantize(gate_codes, gate_scales)
    weight_up = dequantize(up_codes, up_scales)
    grads_all = lax.all_gather(out_grad, "col", axis=0, tiled=True)
    down_partial = jnp.dot(grads_all, weight_down, preferred_element_type=jnp.float32)
    hidden_grad = (
        lax.psum(down_partial.astype(jnp.bfloat16), "row").astype(jnp.float32) * tensor_scales[2]
    )
    gate_rows, up_rows = (
        lax.all_gather(gate_act, "row", axis=0, tiled=True),
        lax.all_gather(up_act, "row", axis=0, tiled=True),
    )
    gate_grad, up_grad = swiglu_grads(hidden_grad, gate_rows, up_rows)
    term = tensor_scales[0] * jnp.dot(gate_grad, weight_gate, preferred_element_type=jnp.float32)
    width_grad = lax.psum_scatter(
        (
            term
            + tensor_scales[1] * jnp.dot(up_grad, weight_up, preferred_element_type=jnp.float32)
        ).astype(jnp.bfloat16),
        "col",
        scatter_dimension=0,
        tiled=True,
    ).astype(jnp.float32)
    largest = lax.pmax(jnp.max(jnp.abs(width_grad)), ("row", "col"))
    grad_unit = (6.0 * width_grad / (largest + 1e-06)).astype(jnp.bfloat16)
    return (grad_unit, largest.reshape(1))


def solution(mesh):
    in_specs = (
        P("col", "row"),
        P("row", "col"),
        P("row", "col"),
        P("col", "row"),
        P("row", "col"),
        P("col", "row"),
        P("row", "col"),
        P("row", "col"),
        P("col", "row"),
        P(),
    )
    out_specs = (P("col", "row"), P())
    return jax.shard_map(
        per_device, mesh=mesh, in_specs=in_specs, out_specs=out_specs, check_vma=False
    )
```

profile of v0, /device:TPU:0, one launch (start us, length us, event | category | flops | bytes accessed | tf_op | source)
XLA Modules:
  0.0 577.6 jit_solution(15263331423390135463)
XLA Ops:
  7.2 0.7 all-gather.4.cloned.1.call-update
  7.9 0.7 all-gather.8.cloned.1.call-update
  8.7 0.7 all-gather.6.cloned.1.call-update
  9.4 7.5 %and_bitcast_fusion.5 = (s32[1024,3696,1]{0,1,2:T(8,128)S(1)}, s32[1024,3696,1]{0,1,2:T(8,128)S(1)}) fusion(s32[1024,3696]{0,1:T(8,128)} %param.17), kind=kLoop, calls=%fused_computation.35 | loop fusion | flops 11354112 | bytes 45416448 | tf_op jit(solution)/shard_map/stack | solution.py:12
  16.9 17.0 %select_multiply_fusion.2 = f32[1024,3696,2]{0,1,2:T(8,128)} fusion(s32[1024,3696,1]{0,1,2:T(8,128)S(1)} %get-tuple-element.5, s32[1024,3696,1]{0,1,2:T(8,128)S(1)} %get-tuple-element.4), kind=kLoop, calls=%fused_computation.11 | loop fusion | flops 121110528 | bytes 60555264 | tf_op jit(solution)/shard_map/mul | solution.py:20
  33.9 50.1 %copy.22 = f32[1024,3696,2]{0,2,1:T(2,128)} copy(f32[1024,3696,2]{0,1,2:T(8,128)} %select_multiply_fusion.2) | data formatting | bytes 60555264 | tf_op jit(solution)/shard_map/mul | solution.py:20
  84.1 37.0 %reshape.101 = f32[1024,7392]{0,1:T(8,128)} reshape(f32[1024,3696,2]{0,2,1:T(2,128)} %copy.22) | data formatting | bytes 60555264 | tf_op jit(solution)/shard_map/mul | solution.py:20
  121.0 0.7 select_bitcast_fusion.2
  121.7 16.5 %fusion.2 = bf16[1024,7392]{0,1:T(8,128)(2,1)} fusion(f32[1024,7392]{0,1:T(8,128)} %reshape.101, f32[1024,462]{0,1:T(8,128)S(1)} %select_bitcast_fusion.2), kind=kLoop, calls=%fused_computation.8 | loop fusion | flops 15138816 | bytes 47308800 | tf_op jit(solution)/shard_map/convert_element_type | solution.py:38
  138.2 7.5 %and_bitcast_fusion.1 = (s32[7392,512,1]{1,0,2:T(8,128)S(1)}, s32[7392,512,1]{1,0,2:T(8,128)S(1)}) fusion(s32[7392,512]{1,0:T(8,128)} %param.15), kind=kLoop, calls=%fused_computation.31 | loop fusion | flops 11354112 | bytes 45416448 | tf_op jit(solution)/shard_map/stack | solution.py:12
  145.7 16.2 %and_bitcast_fusion.3 = (s32[7392,512,1]{1,0,2:T(8,128)}, s32[7392,512,1]{1,0,2:T(8,128)}) fusion(s32[7392,512]{1,0:T(8,128)} %param.13), kind=kLoop, calls=%fused_computation.33 | loop fusion | flops 11354112 | bytes 45416448 | tf_op jit(solution)/shard_map/stack | solution.py:12
  161.9 16.8 %select_multiply_fusion = f32[7392,512,2]{1,0,2:T(8,128)} fusion(s32[7392,512,1]{1,0,2:T(8,128)S(1)} %get-tuple-element.7, s32[7392,512,1]{1,0,2:T(8,128)S(1)} %get-tuple-element.6), kind=kLoop, calls=%fused_computation.9 | loop fusion | flops 121110528 | bytes 60555264 | tf_op jit(solution)/shard_map/mul | solution.py:20
  178.7 18.0 %fusion.11 = bf16[640,7392]{0,1:T(8,128)(2,1)} fusion(bf16[1024,7392]{0,1:T(8,128)(2,1)} %fusion.2, bf16[640,1024]{1,0:T(8,128)(2,1)} %all-gather.4.cloned.1.call-done), kind=kOutput, calls=%fused_computation.37 | convolution fusion | flops 9693573120 | bytes 25911296 | tf_op jit(solution)/shard_map/dot_general | solution.py:68
  196.8 29.2 %select_multiply_fusion.1 = f32[7392,512,2]{1,0,2:T(8,128)} fusion(s32[7392,512,1]{1,0,2:T(8,128)} %get-tuple-element.3, s32[7392,512,1]{1,0,2:T(8,128)} %get-tuple-element.2), kind=kLoop, calls=%fused_computation.10 | loop fusion | flops 121110528 | bytes 60555264 | tf_op jit(solution)/shard_map/mul | solution.py:20
  225.9 45.0 %copy.26 = f32[7392,512,2]{0,2,1:T(2,128)} copy(f32[7392,512,2]{1,0,2:T(8,128)} %select_multiply_fusion) | data formatting | bytes 60555264 | tf_op jit(solution)/shard_map/mul | solution.py:20
  271.0 35.3 %reshape.103 = f32[7392,1024]{0,1:T(8,128)} reshape(f32[7392,512,2]{0,2,1:T(2,128)} %copy.26) | data formatting | bytes 60555264 | tf_op jit(solution)/shard_map/mul | solution.py:20
  306.3 44.9 %copy.25 = f32[7392,512,2]{0,2,1:T(2,128)} copy(f32[7392,512,2]{1,0,2:T(8,128)} %select_multiply_fusion.1) | data formatting | bytes 60555264 | tf_op jit(solution)/shard_map/mul | solution.py:20
  351.2 35.0 %reshape.102 = f32[7392,1024]{0,1:T(8,128)} reshape(f32[7392,512,2]{0,2,1:T(2,128)} %copy.25) | data formatting | bytes 60555264 | tf_op jit(solution)/shard_map/mul | solution.py:20
  386.2 0.7 select_bitcast_fusion
  386.9 18.2 %fusion = bf16[7392,1024]{0,1:T(8,128)(2,1)} fusion(f32[7392,1024]{0,1:T(8,128)} %reshape.103, f32[7392,64]{0,1:T(8,128)S(1)} %select_bitcast_fusion), kind=kLoop, calls=%fused_computation.1 | loop fusion | flops 15138816 | bytes 47308800 | tf_op jit(solution)/shard_map/convert_element_type | solution.py:38
  405.1 0.7 select_bitcast_fusion.1
  405.8 5.5 copy-done
  411.3 7.0 %fusion.1 = bf16[7392,1024]{0,1:T(8,128)(2,1)} fusion(f32[7392,1024]{0,1:T(8,128)S(1)} %copy-done, f32[7392,64]{0,1:T(8,128)S(1)} %select_bitcast_fusion.1), kind=kLoop, calls=%fused_computation.3 | loop fusion | flops 15138816 | bytes 47308800 | tf_op jit(solution)/shard_map/convert_element_type | solution.py:38
  418.3 0.6 fusion.23
  419.0 13.5 %copy.24 = bf16[640,7392]{0,1:T(8,128)(2,1)} copy(bf16[640,7392]{1,0:T(8,128)(2,1)} %all-gather.8.cloned.1.call-done) | data formatting | bytes 18923520 | tf_op jit(solution)/shard_map/all_gather | solution.py:73
  432.5 13.6 %copy.23 = bf16[640,7392]{0,1:T(8,128)(2,1)} copy(bf16[640,7392]{1,0:T(8,128)(2,1)} %all-gather.6.cloned.1.call-done) | data formatting | bytes 18923520 | tf_op jit(solution)/shard_map/all_gather | solution.py:74
  446.1 19.1 %fusion.12 = f32[640,1024]{1,0:T(8,128)S(1)} fusion(bf16[7392,1024]{0,1:T(8,128)(2,1)} %fusion, bf16[640,7392]{0,1:T(8,128)(2,1)} %copy.24, bf16[640,7392]{0,1:T(8,128)(2,1)} %all-reduce.2.cloned.1.call-done, f32[]{:T(128)} %bitcast.6), kind=kOutput, calls=%fused_computation.38 | convolution fusion | flops 9731420160 | bytes 36683780 | tf_op jit(solution)/shard_map/dot_general | solution.py:81
  465.2 27.2 %add_convert_fusion = bf16[640,1024]{1,0:T(8,128)(2,1)} fusion(f32[640,1024]{1,0:T(8,128)S(1)} %fusion.12, bf16[7392,1024]{0,1:T(8,128)(2,1)} %fusion.1, bf16[640,7392]{0,1:T(8,128)(2,1)} %copy.24, bf16[640,7392]{0,1:T(8,128)(2,1)} %copy.23, bf16[640,7392]{0,1:T(8,128)(2,1)} %all-reduce.2.cloned.1.call-done, f32[]{:T(128)} %bitcast.6, f32[]{:T(128)} %bitcast.11, ...), kind=kOutput, calls=%fused_computation.40 | convolution fusion | flops 9757696000 | bytes 47456268 | tf_op jit(solution)/shard_map/dot_general | solution.py:77
  492.5 35.5 %reduce-scatter.2.cloned.1.call-done = bf16[160,1024]{1,0:T(8,128)(2,1)} async-done(((bf16[640,1024]{1,0:T(8,128)(2,1)}), bf16[160,1024]{1,0:T(8,128)(2,1)}) %reduce-scatter.2.cloned.1.call-update) | async-done | bytes 327696 | tf_op jit(solution)/shard_map/reduce_scatter | solution.py:78
  528.0 1.6 fusion.20
  529.6 39.0 %pmax.7 = f32[]{:T(128)} all-reduce(f32[]{:T(128)} %fusion.20), channel_id=1, replica_groups=mesh['row'=8,'col'=4] {'row','col'}, use_global_device_ids=true, to_apply=%region_3.4 | all-reduce | flops 1 | bytes 8 | tf_op jit(solution)/shard_map/pmax | solution.py:87
  569.3 1.8 fusion.19
  (20 shorter events, 0.3 us)
Async XLA Ops:
  7.2 171.6 %all-gather.4.cloned.1.call-start = ((), (), s32[]{:S(2)}) async-start(), calls=%async_computation.1 | async-start | bytes 1638400 | tf_op jit(solution)/shard_map/all_gather | solution.py:67
  7.9 411.1 %all-gather.8.cloned.1.call-start = ((), (), s32[]{:S(2)}) async-start(), calls=%async_computation.4 | async-start | bytes 10690560 | tf_op jit(solution)/shard_map/all_gather | solution.py:73
  8.6 423.9 %all-gather.6.cloned.1.call-start = ((), (), s32[]{:S(2)}) async-start(), calls=%async_computation.3 | async-start | bytes 10690560 | tf_op jit(solution)/shard_map/all_gather | solution.py:74
  9.4 436.7 %all-reduce.2.cloned.1.call-start = ((), (), s32[]{:S(2)}) async-start(), calls=%async_computation.2 | async-start | bytes 18923520 | tf_op jit(solution)/shard_map/psum | solution.py:70
  84.1 37.0 %copy-start.1 = (s32[462,1024]{1,0:T(8,128)S(1)}, s32[462,1024]{1,0:T(8,128)}, u32[]{:S(2)}) copy-start(s32[462,1024]{1,0:T(8,128)} %param.18) | copy-start | bytes 5677060
  196.7 331.3 %reduce-scatter.2.cloned.1.call-start = ((), (), s32[]{:S(2)}) async-start(), calls=%async_computation.5 | async-start | bytes 1638400 | tf_op jit(solution)/shard_map/reduce_scatter | solution.py:78
  351.2 35.0 %copy-start.2 = (s32[64,7392]{1,0:T(8,128)S(1)}, s32[64,7392]{1,0:T(8,128)}, u32[]{:S(2)}) copy-start(s32[64,7392]{1,0:T(8,128)} %param.16) | copy-start | bytes 5677060
  386.9 18.2 %copy-start.3 = (s32[64,7392]{1,0:T(8,128)S(1)}, s32[64,7392]{1,0:T(8,128)}, u32[]{:S(2)}) copy-start(s32[64,7392]{1,0:T(8,128)} %param.14) | copy-start | bytes 5677060
  386.9 24.4 %copy-start = (f32[7392,1024]{0,1:T(8,128)S(1)}, f32[7392,1024]{0,1:T(8,128)}, u32[]{:S(2)}) copy-start(f32[7392,1024]{0,1:T(8,128)} %reshape.102) | copy-start | bytes 90832896
  411.3 7.0 %copy-start.4 = (f32[3]{0:T(128)S(1)}, f32[3]{0:T(128)}, u32[]{:S(2)}) copy-start(f32[3]{0:T(128)} %param.19) | copy-start | bytes 40
Sparse Core Ops, SparseCore 0:
  9.5 35.2 all-gather.3
  46.7 58.0 all-gather.7
  106.7 58.9 all-gather.5
  196.8 142.7 all-reduce.1
  492.6 35.3 reduce-scatter.1
where the time goes:
time: 584 us; the launch traced here: 578 us
  local copies, waits for them, and re-layouts  281 us (48%)
  other arithmetic  141 us (24%)
  matrix products  64.3 us (11%)
  blocking collectives  39 us (7%)
  waiting for transfers between devices  37.6 us (6%)
  between operations  14.5 us (2%)
    mul x6, local copies, waits for them, and re-layouts, fp4_values(): return level * (1.0 - 2.0 * negative)  247 us
    mul x3, other arithmetic, fp4_values(): return level * (1.0 - 2.0 * negative)  63 us
    convert_element_type x3, other arithmetic, dequantize(): return scaled.reshape(row_total, col_total).astype(jnp.bfloat16)  41.6 us
    pmax x1, blocking collectives, per_device(): largest = lax.pmax(jnp.max(jnp.abs(width_grad)), ('row', 'col'))  39 us
    reduce_scatter x1, waiting for transfers between devices, per_device(): lax.psum_scatter((term + tensor_scales[1] * jnp.dot(up_grad, weight_up, p...  35.5 us
    another operation x3, other arithmetic, fp4_values(): jnp.stack([low_bits, high_bits], axis=-1)  31.2 us
    dot_general x1, matrix products, per_device(): jnp.dot(gate_grad, weight_gate, preferred_element_type=jnp.float32)  27.2 us
    dot_general x1, matrix products, per_device(): jnp.dot(up_grad, weight_up, preferred_element_type=jnp.float32)  19.1 us
  transfers between devices with their start and end apart: 5, of which 1 were waited for; matrix products, arithmetic and copies ran while one was open for 75% of the time, Pallas kernels for 0%

commit v1 on v0

v1 whole, which is shorter than its diff:
```python
import functools

import jax
import jax.numpy as jnp
from jax import lax
from jax.experimental import pallas as pl
from jax.experimental.pallas import tpu as pltpu
from jax.sharding import PartitionSpec as P

BLOCK = 16
GROUP = 128
MESH = pl.DeviceIdType.MESH
F32 = jnp.float32
BF16 = jnp.bfloat16


def half_scales(codes):
    exponent = jnp.right_shift(codes, 3)
    mantissa = jnp.bitwise_and(codes, 7)
    units = jnp.where(exponent > 0, jnp.left_shift(8 + mantissa, exponent), 2 * mantissa)
    return (units.astype(F32) * (1.0 / 2048.0)).astype(BF16)


def double_levels(code):
    x = code.astype(F32).astype(BF16)
    negative = x >= 8.0
    m = jnp.where(negative, x - 8.0, x)
    m2 = m + m
    level = jnp.maximum(jnp.maximum(m, m2 - 4.0), m2 + m2 - 16.0)
    return jnp.where(negative, -level, level)


def spread(scales, words):
    blocks = scales.shape[0]
    row = lax.broadcasted_iota(jnp.int32, (blocks, words), 0)
    col = lax.broadcasted_iota(jnp.int32, (blocks, words), 1)
    one_hot = jnp.where(row == jnp.right_shift(col, 3), 1.0, 0.0).astype(BF16)
    return lax.dot_general(
        scales, one_hot, (((0,), (0,)), ((), ())), preferred_element_type=F32
    ).astype(BF16)


def decode(words, scales):
    s = spread(scales, words.shape[1])
    low = double_levels(jnp.bitwise_and(words, 15)) * s
    high = double_levels(jnp.bitwise_and(jnp.right_shift(words, 4), 15)) * s
    return low, high


def split_order(n):
    row = lax.broadcasted_iota(jnp.int32, (n, n), 0)
    col = lax.broadcasted_iota(jnp.int32, (n, n), 1)
    source = jnp.where(col < n // 2, 2 * col, 2 * (col - n // 2) + 1)
    return jnp.where(row == source, 1.0, 0.0).astype(BF16)


def join_order(n):
    row = lax.broadcasted_iota(jnp.int32, (n, n), 0)
    col = lax.broadcasted_iota(jnp.int32, (n, n), 1)
    target = jnp.where(row < n // 2, 2 * row, 2 * (row - n // 2) + 1)
    return jnp.where(col == target, 1.0, 0.0).astype(BF16)


def down_kernel(grad_ref, codes_ref, scale_ref, out_ref):
    low, high = decode(codes_ref[...], scale_ref[...])
    grads = grad_ref[...]
    out_ref[:, :GROUP] = jnp.dot(grads, low, preferred_element_type=F32).astype(BF16)
    out_ref[:, GROUP:] = jnp.dot(grads, high, preferred_element_type=F32).astype(BF16)


def down(grads, codes, scales, groups):
    tokens, width = grads.shape
    return pl.pallas_call(
        down_kernel,
        out_shape=jax.ShapeDtypeStruct((tokens, groups * 2 * GROUP), BF16),
        grid=(groups,),
        in_specs=[
            pl.BlockSpec((tokens, width), lambda i: (0, 0)),
            pl.BlockSpec((width, GROUP), lambda i: (0, i)),
            pl.BlockSpec((GROUP // 8, width), lambda i: (i, 0)),
        ],
        out_specs=pl.BlockSpec((tokens, 2 * GROUP), lambda i: (0, i)),
        compiler_params=pltpu.CompilerParams(vmem_limit_bytes=40 << 20),
        cost_estimate=pl.CostEstimate(
            flops=4 * tokens * width * groups * GROUP,
            bytes_accessed=4 * width * groups * GROUP,
            transcendentals=0,
        ),
    )(grads, codes, scales)


def act_kernel(hidden_units, ts_ref, hidden_ref, gate_ref, up_ref, gg_ref, ug_ref):
    span = 2 * GROUP
    col = lax.broadcasted_iota(jnp.int32, gate_ref.shape, 1) + pl.program_id(0) * span
    inside = col < hidden_units
    to_split, to_natural = split_order(span), join_order(span)
    zero = jnp.zeros(gate_ref.shape, F32)
    gate_in = jnp.where(inside, gate_ref[...].astype(F32), zero).astype(BF16)
    up_in = jnp.where(inside, up_ref[...].astype(F32), zero).astype(BF16)
    g = jnp.dot(gate_in, to_split, preferred_element_type=F32)
    u = jnp.dot(up_in, to_split, preferred_element_type=F32)
    h = hidden_ref[...].astype(F32) * ts_ref[2]
    sig = jax.nn.sigmoid(g)
    gg = (h * u * sig * (1.0 + g * (1.0 - sig))).astype(BF16)
    ug = (h * g * sig).astype(BF16)
    gg_ref[...] = jnp.dot(gg, to_natural, preferred_element_type=F32).astype(BF16)
    ug_ref[...] = jnp.dot(ug, to_natural, preferred_element_type=F32).astype(BF16)


def act(ts, hidden, gate_rows, up_rows):
    rows, padded = hidden.shape
    span = 2 * GROUP
    block = pl.BlockSpec((rows, span), lambda i: (0, i))
    return pl.pallas_call(
        functools.partial(act_kernel, gate_rows.shape[1]),
        out_shape=[jax.ShapeDtypeStruct((rows, padded), BF16)] * 2,
        grid=(padded // span,),
        in_specs=[pl.BlockSpec(memory_space=pltpu.SMEM), block, block, block],
        out_specs=[block, block],
        compiler_params=pltpu.CompilerParams(vmem_limit_bytes=40 << 20),
    )(ts, hidden, gate_rows, up_rows)


def width_kernel(ts_ref, gg_ref, ug_ref, gc_ref, gs_ref, uc_ref, us_ref, out_ref, acc_g, acc_u):
    step = pl.program_id(0)
    half = gc_ref.shape[1]

    @pl.when(step == 0)
    def _():
        acc_g[...] = jnp.zeros_like(acc_g)
        acc_u[...] = jnp.zeros_like(acc_u)

    for grad_ref, code_ref, scale_ref, acc in (
        (gg_ref, gc_ref, gs_ref, acc_g),
        (ug_ref, uc_ref, us_ref, acc_u),
    ):
        low, high = decode(code_ref[...], scale_ref[...])
        grads = grad_ref[...]
        acc[:, :half] += jnp.dot(grads, low, preferred_element_type=F32)
        acc[:, half:] += jnp.dot(grads, high, preferred_element_type=F32)

    @pl.when(step == pl.num_programs(0) - 1)
    def _():
        out_ref[...] = (ts_ref[0] * acc_g[...] + ts_ref[1] * acc_u[...]).astype(BF16)


def width(ts, gg, ug, gate_codes, gate_scales, up_codes, up_scales):
    tokens, padded = gg.shape
    half = gate_codes.shape[1]
    span = 2 * GROUP
    grads = pl.BlockSpec((tokens, span), lambda i: (0, i))
    codes = pl.BlockSpec((span, half), lambda i: (i, 0))
    scales = pl.BlockSpec((half // 8, span), lambda i: (0, i))
    return pl.pallas_call(
        width_kernel,
        out_shape=jax.ShapeDtypeStruct((tokens, 2 * half), BF16),
        grid=(padded // span,),
        in_specs=[
            pl.BlockSpec(memory_space=pltpu.SMEM), grads, grads, codes, scales, codes, scales,
        ],
        out_specs=pl.BlockSpec((tokens, 2 * half), lambda i: (0, 0)),
        scratch_shapes=[pltpu.VMEM((tokens, 2 * half), F32)] * 2,
        compiler_params=pltpu.CompilerParams(vmem_limit_bytes=48 << 20),
    )(ts, gg, ug, gate_codes, gate_scales, up_codes, up_scales)


def finish_kernel(n_row, n_col, q_ref, unit_ref, amax_ref, recv, total, mine, maxes,
                  send, got, max_send, max_got):
    row, col = lax.axis_index("row"), lax.axis_index("col")
    block = total.shape[0]
    col_peers = [(row, lax.rem(col + d, n_col)) for d in range(1, n_col)]
    row_peers = [(lax.rem(row + d, n_row), col) for d in range(1, n_row)]
    barrier = pltpu.get_barrier_semaphore()
    for peer in col_peers + row_peers:
        pl.semaphore_signal(barrier, inc=1, device_id=peer, device_id_type=MESH)
    pl.semaphore_wait(barrier, n_col + n_row - 2)

    copies = []
    for d, peer in enumerate(col_peers):
        start = pl.multiple_of(peer[1] * block, 16)
        copies.append(pltpu.make_async_remote_copy(
            src_ref=q_ref.at[pl.ds(start, block), :], dst_ref=recv.at[d],
            send_sem=send.at[d], recv_sem=got.at[d], device_id=peer, device_id_type=MESH))
    for copy in copies:
        copy.start()
    total[...] = q_ref[pl.ds(pl.multiple_of(col * block, 16), block), :].astype(F32)
    for d, copy in enumerate(copies):
        copy.wait_recv()
        total[...] += recv[d].astype(F32)
    largest = jnp.max(jnp.abs(total[...]))
    mine[0] = jnp.full(mine.shape[1:], largest, F32)

    def exchange(peers, stage, base):
        out = [pltpu.make_async_remote_copy(
            src_ref=mine.at[stage], dst_ref=maxes.at[base + d], send_sem=max_send.at[base + d],
            recv_sem=max_got.at[base + d], device_id=peer, device_id_type=MESH)
            for d, peer in enumerate(peers)]
        for copy in out:
            copy.start()
        value = mine[stage]
        for d, copy in enumerate(out):
            copy.wait_recv()
            value = jnp.maximum(value, maxes[base + d])
        return out, value

    first, value = exchange(col_peers, 0, 0)
    mine[1] = value
    second, value = exchange(row_peers, 1, n_col - 1)
    amax_ref[...] = value
    unit = (6.0 * total[...] / (value[0:1, 0:1] + 1e-6)).astype(BF16)
    unit_ref[...] = jnp.dot(
        unit, join_order(unit.shape[1]), preferred_element_type=F32).astype(BF16)
    for copy in copies + first + second:
        copy.wait_send()


def finish(q, n_row, n_col):
    tokens, width_here = q.shape
    block = tokens // n_col
    peers = n_row + n_col - 2
    vmem = pl.BlockSpec(memory_space=pltpu.VMEM)
    return pl.pallas_call(
        functools.partial(finish_kernel, n_row, n_col),
        out_shape=[
            jax.ShapeDtypeStruct((block, width_here), BF16),
            jax.ShapeDtypeStruct((8, 128), F32),
        ],
        in_specs=[vmem],
        out_specs=[vmem, vmem],
        scratch_shapes=[
            pltpu.VMEM((n_col - 1, block, width_here), BF16),
            pltpu.VMEM((block, width_here), F32),
            pltpu.VMEM((2, 8, 128), F32),
            pltpu.VMEM((peers, 8, 128), F32),
            pltpu.SemaphoreType.DMA((n_col - 1,)),
            pltpu.SemaphoreType.DMA((n_col - 1,)),
            pltpu.SemaphoreType.DMA((peers,)),
            pltpu.SemaphoreType.DMA((peers,)),
        ],
        compiler_params=pltpu.CompilerParams(
            collective_id=3, has_side_effects=True, vmem_limit_bytes=40 << 20),
    )(q)


def per_device(n_row, n_col, out_grad, gate_act, up_act, gate_codes, gate_scales, up_codes,
               up_scales, down_codes, down_scales, ts):
    groups = pl.cdiv(down_codes.shape[1], GROUP)
    extra = groups * GROUP // 8 - down_scales.shape[0]
    ds = jnp.pad(half_scales(down_scales), ((0, extra), (0, 0)))
    more = groups * 2 * GROUP - gate_scales.shape[1]
    gs = jnp.pad(half_scales(gate_scales), ((0, 0), (0, more)))
    us = jnp.pad(half_scales(up_scales), ((0, 0), (0, more)))
    grads = lax.all_gather(out_grad, "col", axis=0, tiled=True)
    partial = down(grads, down_codes, ds, groups)
    hidden = lax.psum_scatter(partial, "row", scatter_dimension=0, tiled=True)
    gg, ug = act(ts, hidden, gate_act, up_act)
    gg = lax.all_gather(gg, "row", axis=0, tiled=True)
    ug = lax.all_gather(ug, "row", axis=0, tiled=True)
    q = width(ts, gg, ug, gate_codes, gs, up_codes, us)
    unit, amax = finish(q, n_row, n_col)
    return unit, amax[0, 0:1]


def solution(mesh):
    n_row, n_col = mesh.shape["row"], mesh.shape["col"]
    in_specs = (
        P("col", "row"), P("row", "col"), P("row", "col"), P("col", "row"), P("row", "col"),
        P("col", "row"), P("row", "col"), P("row", "col"), P("col", "row"), P(),
    )
    return jax.shard_map(
        functools.partial(per_device, n_row, n_col), mesh=mesh, in_specs=in_specs,
        out_specs=(P("col", "row"), P()), check_vma=False,
    )
```

time: 584 us -> 394 us (0.67)
  local copies, waits for them, and re-layouts: 281 us -> 24.9 us
  waiting for transfers between devices: 37.6 us -> 215 us
  other arithmetic: 141 us -> 1.76 us
  Pallas kernels: 0 us -> 138 us
  matrix products: 64.3 us -> 0 us
  blocking collectives: 39 us -> 0 us
    mul x6 -> x0, local copies, waits for them, and re-layouts: 247 us -> none  [fp4_values(): return level * (1.0 - 2.0 * negative)]
    pallas_call x0 -> x4, Pallas kernels: none -> 138 us  [the longest x1 47.2 us: width(): pl.pallas_call(width_kernel, out_shape=jax.ShapeDtypeStruct((tokens, 2 *...]
    all_gather x3, waiting for transfers between devices: 0.01 us -> 137 us  [the longest x1 60.7 us: per_device(): ug = lax.all_gather(ug, 'row', axis=0, tiled=True)]
    dot_general x3 -> x0, matrix products: 64.3 us -> none  [the longest x1 27.2 us: per_device(): jnp.dot(gate_grad, weight_gate, preferred_element_type=jnp.float32)]
    mul x3 -> x0, other arithmetic: 63 us -> none  [fp4_values(): return level * (1.0 - 2.0 * negative)]
    convert_element_type x4 -> x3, other arithmetic: 43.4 us -> 1.76 us  [half_scales(): return (units.astype(F32) * (1.0 / 2048.0)).astype(BF16)]
    reduce_scatter x1, waiting for transfers between devices: 35.5 us -> 76.4 us  [per_device(): hidden = lax.psum_scatter(partial, 'row', scatter_dimension=0, tiled=True)]
    pmax x1 -> x0, blocking collectives: 39 us -> none  [per_device(): largest = lax.pmax(jnp.max(jnp.abs(width_grad)), ('row', 'col'))]
  transfers between devices with their start and end apart: 5 -> 4, of which waited for: 1 -> 4; matrix products, arithmetic and copies ran while one was open for 75% -> 4% of each run, Pallas kernels for 0% -> 0%
where the time goes in v1:
time: 394 us; the launch traced here: 393 us
  waiting for transfers between devices  215 us (55%)
  Pallas kernels  138 us (35%)
  local copies, waits for them, and re-layouts  24.9 us (6%)
  between operations  13.8 us (4%)
    reduce_scatter x1, waiting for transfers between devices, per_device(): hidden = lax.psum_scatter(partial, 'row', scatter_dimension=0, tiled=True)  76.4 us
    all_gather x1, waiting for transfers between devices, per_device(): ug = lax.all_gather(ug, 'row', axis=0, tiled=True)  60.7 us
    all_gather x1, waiting for transfers between devices, per_device(): gg = lax.all_gather(gg, 'row', axis=0, tiled=True)  55.4 us
    pallas_call x1, Pallas kernels, width(): pl.pallas_call(width_kernel, out_shape=jax.ShapeDtypeStruct((tokens, 2 *...  47.2 us
    pallas_call x1, Pallas kernels, finish(): pl.pallas_call(functools.partial(finish_kernel, n_row, n_col), out_shape=...  41.3 us
    pallas_call x1, Pallas kernels, down(): pl.pallas_call(down_kernel, out_shape=jax.ShapeDtypeStruct((tokens, group...  33.6 us
    unnamed x20, local copies, waits for them, and re-layouts  24.2 us
    all_gather x1, waiting for transfers between devices, per_device(): grads = lax.all_gather(out_grad, 'col', axis=0, tiled=True)  20.8 us
  transfers between devices with their start and end apart: 4, of which 4 were waited for; matrix products, arithmetic and copies ran while one was open for 4% of the time, Pallas kernels for 0%

profile of v1, /device:TPU:0, one launch (start us, length us, event | category | flops | bytes accessed | tf_op | source)
XLA Modules:
  0.0 392.8 jit_solution(5525195166853529065)
XLA Ops:
  7.2 0.0 all-gather.4.cloned.1.call-start
  7.2 0.7 all-gather.4.cloned.1.call-update
  7.9 0.0 copy-start.6
  7.9 0.0 reduce-scatter.2.cloned.1.call-start
  8.0 15.4 %copy.12.codes_ref = s32[1024,3696]{1,0:T(8,128)} copy(s32[1024,3696]{0,1:T(8,128)} %param.17) | data formatting | bytes 30277632 | tf_op args[7]
  23.3 0.6 multiply_convert_fusion.2
  23.9 0.1 pad.11.scale_ref
  24.0 20.8 %all-gather.4.cloned.1.call-done.grad_ref = bf16[640,1024]{1,0:T(8,128)(2,1)} async-done(((bf16[160,1024]{1,0:T(8,128)(2,1)}), bf16[640,1024]{1,0:T(8,128)(2,1)}) %all-gather.4.cloned.1.call-update) | async-done | bytes 1310736 | tf_op jit(solution)/shard_map/all_gather | solution.py:253
  44.8 1.3 copy-done.5
  46.1 33.6 %shard_map.113 = bf16[640,7424]{1,0:T(8,128)(2,1)S(1)} custom-call(bf16[640,1024]{1,0:T(8,128)(2,1)S(1)} %copy-done.5, s32[1024,3696]{1,0:T(8,128)} %copy.12.codes_ref, bf16[464,1024]{1,0:T(8,128)(2,1)S(1)} %pad.11.scale_ref), custom_call_target="tpu_custom_call" | custom-call | flops 9730785280 | bytes 15204352 | tf_op jit(solution)/shard_map/pallas_call | solution.py:73
  79.7 0.0 copy-start
  79.7 3.7 copy-done
  83.4 0.0 reduce-scatter.2.cloned.1.call-update
  83.5 0.0 all-gather.6.cloned.1.call-start
  83.5 76.4 %reduce-scatter.2.cloned.1.call-done.hidden_ref = bf16[80,7424]{1,0:T(8,128)(2,1)} async-done(((bf16[640,7424]{1,0:T(8,128)(2,1)}), bf16[80,7424]{1,0:T(8,128)(2,1)}) %reduce-scatter.2.cloned.1.call-update) | async-done | bytes 1187856 | tf_op jit(solution)/shard_map/reduce_scatter | solution.py:255
  159.9 1.3 copy-done.3
  161.2 15.5 %shard_map.114 = (bf16[80,7424]{1,0:T(8,128)(2,1)}, bf16[80,7424]{1,0:T(8,128)(2,1)}) custom-call(f32[3]{0:T(128)S(1)} %copy-done.4, bf16[80,7424]{1,0:T(8,128)(2,1)S(1)} %copy-done.3, bf16[80,7392]{1,0:T(8,128)(2,1)S(1)} %copy-done.1, bf16[80,7392]{1,0:T(8,128)(2,1)S(1)} %copy-done.2), custom_call_target="tpu_custom_call" | custom-call | tf_op jit(solution)/shard_map/pallas_call | solution.py:114
  176.6 0.0 all-gather.6.cloned.1.call-update
  176.7 0.0 all-gather.8.cloned.1.call-start
  176.7 0.5 all-gather.8.cloned.1.call-update
  177.2 0.9 copy-done.7
  178.2 0.6 multiply_convert_fusion.1
  178.7 0.1 pad.12.gs_ref
  178.8 0.9 copy-done.8
  179.7 0.6 multiply_convert_fusion
  180.3 0.1 pad.13.us_ref
  180.3 55.4 %all-gather.6.cloned.1.call-done.gg_ref = bf16[640,7424]{1,0:T(8,128)(2,1)} async-done(((bf16[80,7424]{1,0:T(8,128)(2,1)}), bf16[640,7424]{1,0:T(8,128)(2,1)}) %all-gather.6.cloned.1.call-update) | async-done | bytes 9502736 | tf_op jit(solution)/shard_map/all_gather | solution.py:257
  235.8 60.7 %all-gather.8.cloned.1.call-done.ug_ref = bf16[640,7424]{1,0:T(8,128)(2,1)} async-done(((bf16[80,7424]{1,0:T(8,128)(2,1)}), bf16[640,7424]{1,0:T(8,128)(2,1)}) %all-gather.8.cloned.1.call-update) | async-done | bytes 9502736 | tf_op jit(solution)/shard_map/all_gather | solution.py:258
  296.5 47.2 %shard_map.115.q_ref = bf16[640,1024]{1,0:T(8,128)(2,1)S(1)} custom-call(f32[3]{0:T(128)S(1)} %copy-done.4, bf16[640,7424]{1,0:T(8,128)(2,1)} %all-gather.6.cloned.1.call-done.gg_ref, bf16[640,7424]{1,0:T(8,128)(2,1)} %all-gather.8.cloned.1.call-done.ug_ref, s32[7392,512]{1,0:T(8,128)} %gc_ref.1, bf16[64,7424]{1,0:T(8,128)(2,1)S(1)} %pad.12.gs_ref, ...), custom_call_target="tpu_custom_call" | custom-call | tf_op jit(solution)/shard_map/pallas_call | solution.py:154
  343.7 41.3 %shard_map.116 = (bf16[160,1024]{1,0:T(8,128)(2,1)S(1)}, f32[8,128]{1,0:T(8,128)S(1)}) custom-call(bf16[640,1024]{1,0:T(8,128)(2,1)S(1)} %shard_map.115.q_ref), custom_call_target="tpu_custom_call" | custom-call | tf_op jit(solution)/shard_map/pallas_call | solution.py:222
  385.0 0.5 slice.3
  385.5 0.7 copy.14
  (11 shorter events, 0.0 us)
Async XLA Ops:
  7.2 37.7 %all-gather.4.cloned.1.call-start = ((), (), s32[]{:S(2)}) async-start(), calls=%async_computation.1 | async-start | bytes 1638400 | tf_op jit(solution)/shard_map/all_gather | solution.py:253
  7.9 15.4 %copy-start.6 = (s32[462,1024]{1,0:T(8,128)S(1)}, s32[462,1024]{1,0:T(8,128)}, u32[]{:S(2)}) copy-start(s32[462,1024]{1,0:T(8,128)} %param.18) | copy-start | bytes 5677060
  7.9 152.0 %reduce-scatter.2.cloned.1.call-start = ((), (), s32[]{:S(2)}) async-start(), calls=%async_computation.2 | async-start | bytes 10690560 | tf_op jit(solution)/shard_map/reduce_scatter | solution.py:255
  44.8 1.3 copy-start.5
  79.7 3.7 copy-start
  83.4 76.5 %copy-start.1 = (bf16[80,7392]{1,0:T(8,128)(2,1)S(1)}, bf16[80,7392]{1,0:T(8,128)(2,1)}, u32[]{:S(2)}) copy-start(bf16[80,7392]{1,0:T(8,128)(2,1)} %gate_ref.1) | copy-start | bytes 3548164
  83.4 76.5 %copy-start.2 = (bf16[80,7392]{1,0:T(8,128)(2,1)S(1)}, bf16[80,7392]{1,0:T(8,128)(2,1)}, u32[]{:S(2)}) copy-start(bf16[80,7392]{1,0:T(8,128)(2,1)} %up_ref.1) | copy-start | bytes 3548164
  83.4 76.5 %copy-start.4 = (f32[3]{0:T(128)S(1)}, f32[3]{0:T(128)}, u32[]{:S(2)}) copy-start(f32[3]{0:T(128)} %ts_ref.3) | copy-start | bytes 40
  83.5 152.3 %all-gather.6.cloned.1.call-start = ((), (), s32[]{:S(2)}) async-start(), calls=%async_computation.3 | async-start | bytes 10690560 | tf_op jit(solution)/shard_map/all_gather | solution.py:257
  159.9 1.3 copy-start.3
  176.6 1.5 copy-start.7
  176.7 119.9 %all-gather.8.cloned.1.call-start = ((), (), s32[]{:S(2)}) async-start(), calls=%async_computation.4 | async-start | bytes 10690560 | tf_op jit(solution)/shard_map/all_gather | solution.py:258
  178.2 1.5 copy-start.8
Sparse Core Ops, SparseCore 0:
  9.5 35.2 all-gather.3
  83.6 76.2 reduce-scatter.1
  176.8 58.9 all-gather.5
  237.5 58.9 all-gather.7

commit v2 on v1

v2 whole, which is shorter than its diff:
```python
import functools

import jax
import jax.numpy as jnp
from jax import lax
from jax.experimental import pallas as pl
from jax.experimental.pallas import tpu as pltpu
from jax.sharding import PartitionSpec as P

BLOCK = 16
SPAN = 512
GROUP = 128
MESH = pl.DeviceIdType.MESH
F32 = jnp.float32
BF16 = jnp.bfloat16


def half_scales(codes):
    exponent = jnp.right_shift(codes, 3)
    mantissa = jnp.bitwise_and(codes, 7)
    units = jnp.where(exponent > 0, jnp.left_shift(8 + mantissa, exponent), 2 * mantissa)
    return (units.astype(F32) * (1.0 / 2048.0)).astype(BF16)


def double_levels(code):
    x = code.astype(F32).astype(BF16)
    negative = x >= 8.0
    m = jnp.where(negative, x - 8.0, x)
    m2 = m + m
    level = jnp.maximum(jnp.maximum(m, m2 - 4.0), m2 + m2 - 16.0)
    return jnp.where(negative, -level, level)


def spread(scales, words):
    blocks = scales.shape[0]
    row = lax.broadcasted_iota(jnp.int32, (blocks, words), 0)
    col = lax.broadcasted_iota(jnp.int32, (blocks, words), 1)
    one_hot = jnp.where(row == jnp.right_shift(col, 3), 1.0, 0.0).astype(BF16)
    return lax.dot_general(
        scales, one_hot, (((0,), (0,)), ((), ())), preferred_element_type=F32
    ).astype(BF16)


def decode(words, scales):
    s = spread(scales, words.shape[1])
    low = double_levels(jnp.bitwise_and(words, 15)) * s
    high = double_levels(jnp.bitwise_and(jnp.right_shift(words, 4), 15)) * s
    return low, high


def split_order(n):
    row = lax.broadcasted_iota(jnp.int32, (n, n), 0)
    col = lax.broadcasted_iota(jnp.int32, (n, n), 1)
    source = jnp.where(col < n // 2, 2 * col, 2 * (col - n // 2) + 1)
    return jnp.where(row == source, 1.0, 0.0).astype(BF16)


def join_order(n):
    row = lax.broadcasted_iota(jnp.int32, (n, n), 0)
    col = lax.broadcasted_iota(jnp.int32, (n, n), 1)
    target = jnp.where(row < n // 2, 2 * row, 2 * (row - n // 2) + 1)
    return jnp.where(col == target, 1.0, 0.0).astype(BF16)


def down_kernel(grad_ref, codes_ref, scale_ref, out_ref):
    low, high = decode(codes_ref[...], scale_ref[...])
    grads = grad_ref[...]
    out_ref[:, :GROUP] = jnp.dot(grads, low, preferred_element_type=F32).astype(BF16)
    out_ref[:, GROUP:] = jnp.dot(grads, high, preferred_element_type=F32).astype(BF16)


def down(grads, codes, scales, groups):
    tokens, width = grads.shape
    return pl.pallas_call(
        down_kernel,
        out_shape=jax.ShapeDtypeStruct((tokens, groups * 2 * GROUP), BF16),
        grid=(groups,),
        in_specs=[
            pl.BlockSpec((tokens, width), lambda i: (0, 0)),
            pl.BlockSpec((width, GROUP), lambda i: (0, i)),
            pl.BlockSpec((GROUP // 8, width), lambda i: (i, 0)),
        ],
        out_specs=pl.BlockSpec((tokens, 2 * GROUP), lambda i: (0, i)),
        compiler_params=pltpu.CompilerParams(vmem_limit_bytes=40 << 20),
        cost_estimate=pl.CostEstimate(
            flops=4 * tokens * width * groups * GROUP,
            bytes_accessed=4 * width * groups * GROUP,
            transcendentals=0,
        ),
    )(grads, codes, scales)


def act_kernel(hidden_units, ts_ref, hidden_ref, gate_ref, up_ref, out_ref):
    span, unit = gate_ref.shape[1], 2 * GROUP
    to_split, to_natural = split_order(unit), join_order(unit)
    for part in range(span // unit):
        cols = slice(part * unit, (part + 1) * unit)
        shape = (gate_ref.shape[0], unit)
        col = lax.broadcasted_iota(jnp.int32, shape, 1) + pl.program_id(0) * span + part * unit
        inside = col < hidden_units
        zero = jnp.zeros(shape, F32)
        gate_in = jnp.where(inside, gate_ref[:, cols].astype(F32), zero).astype(BF16)
        up_in = jnp.where(inside, up_ref[:, cols].astype(F32), zero).astype(BF16)
        g = jnp.dot(gate_in, to_split, preferred_element_type=F32)
        u = jnp.dot(up_in, to_split, preferred_element_type=F32)
        h = hidden_ref[:, cols].astype(F32) * ts_ref[2]
        sig = jax.nn.sigmoid(g)
        gg = (h * u * sig * (1.0 + g * (1.0 - sig))).astype(BF16)
        ug = (h * g * sig).astype(BF16)
        gg = jnp.dot(gg, to_natural, preferred_element_type=F32)
        ug = jnp.dot(ug, to_natural, preferred_element_type=F32)
        out_ref[0, 0, :, cols] = jnp.where(inside, gg, zero).astype(BF16)
        out_ref[0, 1, :, cols] = jnp.where(inside, ug, zero).astype(BF16)


def act(ts, hidden, gate_rows, up_rows, steps):
    rows = hidden.shape[0]
    block = pl.BlockSpec((rows, SPAN), lambda i: (0, i))
    return pl.pallas_call(
        functools.partial(act_kernel, gate_rows.shape[1]),
        out_shape=jax.ShapeDtypeStruct((steps, 2, rows, SPAN), BF16),
        grid=(steps,),
        in_specs=[pl.BlockSpec(memory_space=pltpu.SMEM), block, block, block],
        out_specs=pl.BlockSpec((1, 2, rows, SPAN), lambda i: (i, 0, 0, 0)),
        compiler_params=pltpu.CompilerParams(vmem_limit_bytes=40 << 20),
    )(ts, hidden, gate_rows, up_rows)


LAG = 2


def width_kernel(n_row, n_col, steps, ts_ref, own_ref, gc_ref, gs_ref, uc_ref, us_ref,
                 unit_ref, amax_ref, held, acc_g, acc_u, q_buf, recv, total, mine, maxes,
                 own_sem, far_send, far_got, hop_send, hop_got, near_send, near_got,
                 send, got, max_send, max_got):
    step = pl.program_id(0)
    half = gc_ref.shape[1]
    row, col = lax.axis_index("row"), lax.axis_index("col")
    chips = n_row // 2
    chip, core = row // 2, lax.rem(row, 2)
    relay = chips == 4
    partner = (chip * 2 + (1 - core), col)
    block = total.shape[0]
    col_peers = [(row, lax.rem(col + d, n_col)) for d in range(1, n_col)]
    row_peers = [(lax.rem(row + d, n_row), col) for d in range(1, n_row)]

    def other(q):
        flipped = chip
        bit = 1
        while bit < chips:
            if q & bit:
                flipped = flipped + bit - 2 * bit * lax.rem(chip // bit, 2)
            bit *= 2
        return flipped

    direct = (1, 2) if relay else tuple(range(1, chips))
    peer_of = {q: (other(q) * 2 + core, col) for q in range(1, chips)}
    row_of = {q: other(q) * 2 + core for q in range(1, chips)}
    row_of[0] = row

    def own_copy(j):
        return pltpu.make_async_copy(own_ref.at[j], held.at[j, row], own_sem.at[j])

    def far_copy(j, q):
        return pltpu.make_async_remote_copy(
            src_ref=own_ref.at[j], dst_ref=held.at[j, row], send_sem=far_send.at[j, q],
            recv_sem=far_got.at[j, q], device_id=peer_of[q], device_id_type=MESH)

    def hop_copy(j, h):
        source, target = (1, 2) if h == 0 else (2, 1)
        return pltpu.make_async_remote_copy(
            src_ref=held.at[j, row_of[source], h], dst_ref=held.at[j, row_of[source], h],
            send_sem=hop_send.at[j, h], recv_sem=hop_got.at[j, h],
            device_id=peer_of[target], device_id_type=MESH)

    def near_copy(j, q):
        src = own_ref.at[j] if q == 0 else held.at[j, row_of[q]]
        return pltpu.make_async_remote_copy(
            src_ref=src, dst_ref=held.at[j, row_of[q]], send_sem=near_send.at[j, q],
            recv_sem=near_got.at[j, q], device_id=partner, device_id_type=MESH)

    @pl.when(step == 0)
    def _():
        barrier = pltpu.get_barrier_semaphore()
        for peer in col_peers + row_peers:
            pl.semaphore_signal(barrier, inc=1, device_id=peer, device_id_type=MESH)
        pl.semaphore_wait(barrier, n_col + n_row - 2)

        @pl.loop(0, steps)
        def _(j):
            for q in direct:
                far_copy(j, q).start()
            near_copy(j, 0).start()
            own_copy(j).start()

        acc_g[...] = jnp.zeros_like(acc_g)
        acc_u[...] = jnp.zeros_like(acc_u)

    @pl.when(step < steps)
    def _():
        for q in direct:
            far_copy(step, q).wait_recv()
            if relay:
                hop_copy(step, q - 1).start()
            near_copy(step, q).start()

    if relay:
        @pl.when(jnp.logical_and(step >= 1, step < steps + 1))
        def _():
            for h in range(2):
                hop_copy(step - 1, h).wait_recv()
            near_copy(step - 1, 3).start()

    @pl.when(step >= LAG)
    def _():
        j = step - LAG
        own_copy(j).wait()
        for q in range(chips):
            near_copy(j, q).wait_recv()
        for part, code_ref, scale_ref, acc in (
            (0, gc_ref, gs_ref, acc_g),
            (1, uc_ref, us_ref, acc_u),
        ):
            low, high = decode(code_ref[...], scale_ref[...])
            grads = held[j, :, part].reshape(acc.shape[0], SPAN)
            acc[:, :half] += jnp.dot(grads, low, preferred_element_type=F32)
            acc[:, half:] += jnp.dot(grads, high, preferred_element_type=F32)

    @pl.when(step == steps + LAG - 1)
    def _():
        q_buf[...] = (ts_ref[0] * acc_g[...] + ts_ref[1] * acc_u[...]).astype(BF16)
        copies = []
        for d, peer in enumerate(col_peers):
            start = pl.multiple_of(peer[1] * block, 16)
            copies.append(pltpu.make_async_remote_copy(
                src_ref=q_buf.at[pl.ds(start, block), :], dst_ref=recv.at[d],
                send_sem=send.at[d], recv_sem=got.at[d], device_id=peer, device_id_type=MESH))
        for copy in copies:
            copy.start()
        total[...] = q_buf[pl.ds(pl.multiple_of(col * block, 16), block), :].astype(F32)
        for d, copy in enumerate(copies):
            copy.wait_recv()
            total[...] += recv[d].astype(F32)
        largest = jnp.max(jnp.abs(total[...]))
        mine[0] = jnp.full(mine.shape[1:], largest, F32)

        def exchange(peers, stage, base):
            out = [pltpu.make_async_remote_copy(
                src_ref=mine.at[stage], dst_ref=maxes.at[base + d],
                send_sem=max_send.at[base + d], recv_sem=max_got.at[base + d],
                device_id=peer, device_id_type=MESH) for d, peer in enumerate(peers)]
            for copy in out:
                copy.start()
            value = mine[stage]
            for d, copy in enumerate(out):
                copy.wait_recv()
                value = jnp.maximum(value, maxes[base + d])
            return out, value

        first, value = exchange(col_peers, 0, 0)
        mine[1] = value
        second, value = exchange(row_peers, 1, n_col - 1)
        amax_ref[...] = value
        unit = (6.0 * total[...] / (value[0:1, 0:1] + 1e-6)).astype(BF16)
        unit_ref[...] = jnp.dot(
            unit, join_order(unit.shape[1]), preferred_element_type=F32).astype(BF16)
        for copy in copies + first + second:
            copy.wait_send()

        @pl.loop(0, steps)
        def _(j):
            for q in direct:
                far_copy(j, q).wait_send()
                if relay:
                    hop_copy(j, q - 1).wait_send()
            for q in range(chips):
                near_copy(j, q).wait_send()


def width(ts, own, gate_codes, gate_scales, up_codes, up_scales, n_row, n_col):
    steps, _, rows, _ = own.shape
    half = gate_codes.shape[1]
    tokens, chips, peers = rows * n_row, n_row // 2, n_row + n_col - 2
    block = tokens // n_col
    codes = pl.BlockSpec((SPAN, half), lambda i: (jnp.maximum(i - LAG, 0), 0))
    scales = pl.BlockSpec((half // 8, SPAN), lambda i: (0, jnp.maximum(i - LAG, 0)))
    dma = pltpu.SemaphoreType.DMA
    return pl.pallas_call(
        functools.partial(width_kernel, n_row, n_col, steps),
        out_shape=[
            jax.ShapeDtypeStruct((block, 2 * half), BF16),
            jax.ShapeDtypeStruct((8, 128), F32),
        ],
        grid=(steps + LAG,),
        in_specs=[
            pl.BlockSpec(memory_space=pltpu.SMEM), pl.BlockSpec(memory_space=pl.ANY),
            codes, scales, codes, scales,
        ],
        out_specs=[
            pl.BlockSpec((block, 2 * half), lambda i: (0, 0)),
            pl.BlockSpec((8, 128), lambda i: (0, 0)),
        ],
        scratch_shapes=[
            pltpu.VMEM((steps, n_row, 2, rows, SPAN), BF16),
            pltpu.VMEM((tokens, 2 * half), F32),
            pltpu.VMEM((tokens, 2 * half), F32),
            pltpu.VMEM((tokens, 2 * half), BF16),
            pltpu.VMEM((n_col - 1, block, 2 * half), BF16),
            pltpu.VMEM((block, 2 * half), F32),
            pltpu.VMEM((2, 8, 128), F32),
            pltpu.VMEM((peers, 8, 128), F32),
            dma((steps,)),
            dma((steps, chips)),
            dma((steps, chips)),
            dma((steps, 2)),
            dma((steps, 2)),
            dma((steps, chips)),
            dma((steps, chips)),
            dma((n_col - 1,)),
            dma((n_col - 1,)),
            dma((peers,)),
            dma((peers,)),
        ],
        compiler_params=pltpu.CompilerParams(
            collective_id=3, has_side_effects=True, vmem_limit_bytes=60 << 20,
            dimension_semantics=("arbitrary",)),
    )(ts, own, gate_codes, gate_scales, up_codes, up_scales)


def per_device(n_row, n_col, out_grad, gate_act, up_act, gate_codes, gate_scales, up_codes,
               up_scales, down_codes, down_scales, ts):
    groups = pl.cdiv(down_codes.shape[1], GROUP)
    extra = groups * GROUP // 8 - down_scales.shape[0]
    ds = jnp.pad(half_scales(down_scales), ((0, extra), (0, 0)))
    steps = pl.cdiv(gate_scales.shape[1], SPAN)
    more = steps * SPAN - gate_scales.shape[1]
    gs = jnp.pad(half_scales(gate_scales), ((0, 0), (0, more)))
    us = jnp.pad(half_scales(up_scales), ((0, 0), (0, more)))
    grads = lax.all_gather(out_grad, "col", axis=0, tiled=True)
    partial = down(grads, down_codes, ds, groups)
    hidden = lax.psum_scatter(partial, "row", scatter_dimension=0, tiled=True)
    own = act(ts, hidden, gate_act, up_act, steps)
    unit, amax = width(ts, own, gate_codes, gs, up_codes, us, n_row, n_col)
    return unit, amax[0, 0:1]


def solution(mesh):
    n_row, n_col = mesh.shape["row"], mesh.shape["col"]
    in_specs = (
        P("col", "row"), P("row", "col"), P("row", "col"), P("col", "row"), P("row", "col"),
        P("col", "row"), P("row", "col"), P("row", "col"), P("col", "row"), P(),
    )
    return jax.shard_map(
        functools.partial(per_device, n_row, n_col), mesh=mesh, in_specs=in_specs,
        out_specs=(P("col", "row"), P()), check_vma=False,
    )
```

time: 394 us -> 331 us (0.84)
  waiting for transfers between devices: 215 us -> 93.1 us
  Pallas kernels: 138 us -> 192 us
  local copies, waits for them, and re-layouts: 24.9 us -> 29.7 us
    all_gather x2 -> x0, waiting for transfers between devices: 116 us -> none  [the longest x1 60.7 us: per_device(): ug = lax.all_gather(ug, 'row', axis=0, tiled=True)]
    pallas_call x2 -> x1, Pallas kernels: 88.5 us -> 148 us  [width(): pl.pallas_call(functools.partial(width_kernel, n_row, n_col, steps), out_...]
    pallas_call x1, Pallas kernels: 15.5 us -> 9.64 us  [act(): pl.pallas_call(functools.partial(act_kernel, gate_rows.shape[1]), out_sha...]
    reduce_scatter x1, waiting for transfers between devices: 76.4 us -> 71.7 us  [per_device(): hidden = lax.psum_scatter(partial, 'row', scatter_dimension=0, tiled=True)]
    unnamed x20 -> x22, local copies, waits for them, and re-layouts: 24.2 us -> 26.4 us
  transfers between devices with their start and end apart: 4 -> 2, of which waited for: 4 -> 2; matrix products, arithmetic and copies ran while one was open for 4% -> 6% of each run, Pallas kernels for 0% -> 0%
where the time goes in v2:
time: 331 us
  Pallas kernels  192 us (58%)
  waiting for transfers between devices  93.1 us (28%)
  local copies, waits for them, and re-layouts  29.7 us (9%)
  between operations  14.1 us (4%)
    pallas_call x1, Pallas kernels, width(): pl.pallas_call(functools.partial(width_kernel, n_row, n_col, steps), out_...  148 us
    reduce_scatter x1, waiting for transfers between devices, per_device(): hidden = lax.psum_scatter(partial, 'row', scatter_dimension=0, tiled=True)  71.7 us
    pallas_call x1, Pallas kernels, down(): pl.pallas_call(down_kernel, out_shape=jax.ShapeDtypeStruct((tokens, group...  33.8 us
    unnamed x22, local copies, waits for them, and re-layouts  26.4 us
    all_gather x1, waiting for transfers between devices, per_device(): grads = lax.all_gather(out_grad, 'col', axis=0, tiled=True)  20.8 us
    pallas_call x1, Pallas kernels, act(): pl.pallas_call(functools.partial(act_kernel, gate_rows.shape[1]), out_sha...  9.64 us
  transfers between devices with their start and end apart: 2, of which 2 were waited for; matrix products, arithmetic and copies ran while one was open for 6% of the time, Pallas kernels for 0%

profile of v2, /device:TPU:0, one launch (start us, length us, event | category | flops | bytes accessed | tf_op | source)
XLA Modules:
  0.0 330.6 jit_solution(3426832938565487158)
XLA Ops:
  7.2 0.0 all-gather.2.cloned.1.call-start
  7.2 0.7 all-gather.2.cloned.1.call-update
  7.9 0.0 copy-start.7
  7.9 0.0 reduce-scatter.2.cloned.1.call-start
  8.0 15.4 %copy.12.codes_ref = s32[1024,3696]{1,0:T(8,128)} copy(s32[1024,3696]{0,1:T(8,128)} %param.17) | data formatting | bytes 30277632 | tf_op args[7]
  23.4 0.0 copy-done.7
  23.4 0.6 multiply_convert_fusion.2
  24.0 0.1 pad.11.scale_ref
  24.1 20.8 %all-gather.2.cloned.1.call-done.grad_ref = bf16[640,1024]{1,0:T(8,128)(2,1)} async-done(((bf16[160,1024]{1,0:T(8,128)(2,1)}), bf16[640,1024]{1,0:T(8,128)(2,1)}) %all-gather.2.cloned.1.call-update) | async-done | bytes 1310736 | tf_op jit(solution)/shard_map/all_gather | solution.py:339
  44.8 0.0 copy-start.6
  44.8 1.3 copy-done.6
  46.1 33.8 %shard_map.113 = bf16[640,7424]{1,0:T(8,128)(2,1)S(1)} custom-call(bf16[640,1024]{1,0:T(8,128)(2,1)S(1)} %copy-done.6, s32[1024,3696]{1,0:T(8,128)} %copy.12.codes_ref, bf16[464,1024]{1,0:T(8,128)(2,1)S(1)} %pad.11.scale_ref), custom_call_target="tpu_custom_call" | custom-call | flops 9730785280 | bytes 15204352 | tf_op jit(solution)/shard_map/pallas_call | solution.py:74
  79.9 0.0 copy-start.1
  79.9 3.7 %copy-done.1 = bf16[640,7424]{1,0:T(8,128)(2,1)} copy-done((bf16[640,7424]{1,0:T(8,128)(2,1)}, bf16[640,7424]{1,0:T(8,128)(2,1)S(1)}, u32[]{:S(2)}) %copy-start.1) | copy-done | bytes 9502744
  83.6 0.0 reduce-scatter.2.cloned.1.call-update
  83.6 1.5 copy-done.8
  85.1 0.6 multiply_convert_fusion.1
  85.7 1.0 pad.12.gs_ref
  86.7 0.0 copy-done.9
  86.7 0.6 multiply_convert_fusion
  87.3 1.0 pad.13.us_ref
  88.4 71.7 %reduce-scatter.2.cloned.1.call-done.hidden_ref = bf16[80,7424]{1,0:T(8,128)(2,1)} async-done(((bf16[640,7424]{1,0:T(8,128)(2,1)}), bf16[80,7424]{1,0:T(8,128)(2,1)}) %reduce-scatter.2.cloned.1.call-update) | async-done | bytes 1187856 | tf_op jit(solution)/shard_map/reduce_scatter | solution.py:341
  160.0 0.0 copy-done.2
  160.0 0.0 copy-done.3
  160.0 0.0 copy-done.5
  160.1 1.3 copy-done.4
  161.3 9.6 %shard_map.114.own_ref = bf16[15,2,80,512]{3,2,1,0:T(8,128)(2,1)S(1)} custom-call(f32[3]{0:T(128)S(1)} %copy-done.5, bf16[80,7424]{1,0:T(8,128)(2,1)S(1)} %copy-done.4, bf16[80,7392]{1,0:T(8,128)(2,1)S(1)} %copy-done.2, bf16[80,7392]{1,0:T(8,128)(2,1)S(1)} %copy-done.3), custom_call_target="tpu_custom_call" | custom-call | tf_op jit(solution)/shard_map/pallas_call | solution.py:119
  171.0 0.0 copy-start
  171.0 1.4 copy-done
  172.4 148.4 %shard_map.115 = (bf16[160,1024]{1,0:T(8,128)(2,1)}, f32[8,128]{1,0:T(8,128)}) custom-call(f32[3]{0:T(128)} %ts_ref.3, bf16[15,2,80,512]{3,2,1,0:T(8,128)(2,1)} %copy-done, s32[7392,512]{1,0:T(8,128)} %gc_ref.1, bf16[64,7680]{1,0:T(8,128)(2,1)} %pad.12.gs_ref, s32[7392,512]{1,0:T(8,128)} %uc_ref.1, bf16[64,7680]{1,0:T(8,128)(2,1)} %pad.13.us_ref), custom_call_target="tpu_custom_call" | custom-call | tf_op jit(solution)/shard_map/pallas_call | solution.py:288
  320.8 1.2 slice.3
  322.0 1.7 copy.14
  (6 shorter events, 0.0 us)
Async XLA Ops:
  7.2 37.7 %all-gather.2.cloned.1.call-start = ((), (), s32[]{:S(2)}) async-start(), calls=%async_computation.1 | async-start | bytes 1638400 | tf_op jit(solution)/shard_map/all_gather | solution.py:339
  7.9 15.5 %copy-start.7 = (s32[462,1024]{1,0:T(8,128)S(1)}, s32[462,1024]{1,0:T(8,128)}, u32[]{:S(2)}) copy-start(s32[462,1024]{1,0:T(8,128)} %param.18) | copy-start | bytes 5677060
  7.9 152.1 %reduce-scatter.2.cloned.1.call-start = ((), (), s32[]{:S(2)}) async-start(), calls=%async_computation.2 | async-start | bytes 10690560 | tf_op jit(solution)/shard_map/reduce_scatter | solution.py:341
  44.8 1.3 copy-start.6
  79.9 3.7 %copy-start.1 = (bf16[640,7424]{1,0:T(8,128)(2,1)}, bf16[640,7424]{1,0:T(8,128)(2,1)S(1)}, u32[]{:S(2)}) copy-start(bf16[640,7424]{1,0:T(8,128)(2,1)S(1)} %shard_map.113) | copy-start | bytes 28508164
  83.6 1.5 copy-start.8
  85.1 1.6 copy-start.9
  86.7 73.3 %copy-start.2 = (bf16[80,7392]{1,0:T(8,128)(2,1)S(1)}, bf16[80,7392]{1,0:T(8,128)(2,1)}, u32[]{:S(2)}) copy-start(bf16[80,7392]{1,0:T(8,128)(2,1)} %gate_ref.1) | copy-start | bytes 3548164
  86.7 73.3 %copy-start.3 = (bf16[80,7392]{1,0:T(8,128)(2,1)S(1)}, bf16[80,7392]{1,0:T(8,128)(2,1)}, u32[]{:S(2)}) copy-start(bf16[80,7392]{1,0:T(8,128)(2,1)} %up_ref.1) | copy-start | bytes 3548164
  86.7 73.3 %copy-start.5 = (f32[3]{0:T(128)S(1)}, f32[3]{0:T(128)}, u32[]{:S(2)}) copy-start(f32[3]{0:T(128)} %ts_ref.3) | copy-start | bytes 40
  160.0 1.3 copy-start.4
  171.0 1.4 copy-start
Sparse Core Ops, SparseCore 0:
  9.5 35.2 all-gather.1
  83.7 76.2 reduce-scatter.1

commit v3 on v2

--- a/solution.py
+++ b/solution.py
@@ -62,32 +62,139 @@
     return jnp.where(col == target, 1.0, 0.0).astype(BF16)
 
 
-def down_kernel(grad_ref, codes_ref, scale_ref, out_ref):
-    low, high = decode(codes_ref[...], scale_ref[...])
-    grads = grad_ref[...]
-    out_ref[:, :GROUP] = jnp.dot(grads, low, preferred_element_type=F32).astype(BF16)
-    out_ref[:, GROUP:] = jnp.dot(grads, high, preferred_element_type=F32).astype(BF16)
-
-
-def down(grads, codes, scales, groups):
-    tokens, width = grads.shape
+def decode_rows(words, scales):
+    blocks, wide = scales.shape
+    s = jnp.broadcast_to(scales.astype(F32)[:, None, :], (blocks, 8, wide))
+    s = s.reshape(blocks * 8, wide).astype(BF16)
+    low = double_levels(jnp.bitwise_and(words, 15)) * s
+    high = double_levels(jnp.bitwise_and(jnp.right_shift(words, 4), 15)) * s
+    return low, high
+
+
+def flip(chip, q, chips):
+    flipped = chip
+    bit = 1
+    while bit < chips:
+        if q & bit:
+            flipped = flipped + bit - 2 * bit * lax.rem(chip // bit, 2)
+        bit *= 2
+    return flipped
+
+
+DOWN_LAG = 4
+
+
+def down_kernel(n_row, n_col, groups, own_ref, codes_ref, scale_ref, out_ref, grads, parts,
+                near, sums, far, own_sem, all_send, all_got, near_send, near_got, far_send,
+                far_got):
+    step = pl.program_id(0)
+    row, col = lax.axis_index("row"), lax.axis_index("col")
+    chips = n_row // 2
+    chip, core = row // 2, lax.rem(row, 2)
+    partner = (chip * 2 + (1 - core), col)
+    rows, span = out_ref.shape
+    col_peers = [(row, lax.rem(col + d, n_col)) for d in range(1, n_col)]
+    peers = [(flip(chip, q, chips) * 2 + core, col) for q in range(1, chips)]
+
+    def near_copy(j):
+        return pltpu.make_async_remote_copy(
+            src_ref=parts.at[j, 1 - core], dst_ref=near.at[j], send_sem=near_send.at[j],
+            recv_sem=near_got.at[j], device_id=partner, device_id_type=MESH)
+
+    def far_copy(j, q):
+        return pltpu.make_async_remote_copy(
+            src_ref=sums.at[j, flip(chip, q, chips)], dst_ref=far.at[j, q - 1],
+            send_sem=far_send.at[j, q - 1], recv_sem=far_got.at[j, q - 1],
+            device_id=peers[q - 1], device_id_type=MESH)
+
+    @pl.when(step == 0)
+    def _():
+        barrier = pltpu.get_barrier_semaphore()
+        for peer in col_peers + peers + [partner]:
+            pl.semaphore_signal(barrier, inc=1, device_id=peer, device_id_type=MESH)
+        pl.semaphore_wait(barrier, n_col - 1 + chips)
+        copies = [pltpu.make_async_remote_copy(
+            src_ref=own_ref, dst_ref=grads.at[col], send_sem=all_send.at[d],
+            recv_sem=all_got.at[d], device_id=peer, device_id_type=MESH)
+            for d, peer in enumerate(col_peers)]
+        for copy in copies:
+            copy.start()
+        mine = pltpu.make_async_copy(own_ref, grads.at[col], own_sem)
+        mine.start()
+        mine.wait()
+        for copy in copies:
+            copy.wait()
+
+    @pl.when(step < groups)
+    def _():
+        low, high = decode_rows(codes_ref[...], scale_ref[...])
+        left = grads[...].reshape(n_row * rows, grads.shape[2])
+        for h, weight in enumerate((low, high)):
+            part = lax.dot_general(
+                left, weight, (((1,), (1,)), ((), ())), preferred_element_type=F32
+            ).astype(BF16).reshape(chips, 2, rows, GROUP)
+            for c in range(2):
+                parts[step, c, :, :, h * GROUP:(h + 1) * GROUP] = part[:, c]
+        near_copy(step).start()
+
+    @pl.when(jnp.logical_and(step >= 1, step <= groups))
+    def _():
+        j = step - 1
+        near_copy(j).wait_recv()
+        sums[j] = (parts[j, core].astype(F32) + near[j].astype(F32)).astype(BF16)
+        for q in range(1, chips):
+            far_copy(j, q).start()
+
+    @pl.when(step >= DOWN_LAG)
+    def _():
+        j = step - DOWN_LAG
+        value = sums[j, chip].astype(F32)
+        for q in range(1, chips):
+            far_copy(j, q).wait_recv()
+            value = value + far[j, q - 1].astype(F32)
+        out_ref[...] = value
+
+    @pl.when(step == groups + DOWN_LAG - 1)
+    def _():
+        @pl.loop(0, groups)
+        def _(j):
+            near_copy(j).wait_send()
+            for q in range(1, chips):
+                far_copy(j, q).wait_send()
+
+
+def down(out_grad, codes, scales, groups, n_row, n_col):
+    here, wide = out_grad.shape
+    rows, chips, span = here * n_col // n_row, n_row // 2, 2 * GROUP
+    dma = pltpu.SemaphoreType.DMA
     return pl.pallas_call(
-        down_kernel,
-        out_shape=jax.ShapeDtypeStruct((tokens, groups * 2 * GROUP), BF16),
-        grid=(groups,),
+        functools.partial(down_kernel, n_row, n_col, groups),
+        out_shape=jax.ShapeDtypeStruct((rows, groups * span), F32),
+        grid=(groups + DOWN_LAG,),
         in_specs=[
-            pl.BlockSpec((tokens, width), lambda i: (0, 0)),
-            pl.BlockSpec((width, GROUP), lambda i: (0, i)),
-            pl.BlockSpec((GROUP // 8, width), lambda i: (i, 0)),
-        ],
-        out_specs=pl.BlockSpec((tokens, 2 * GROUP), lambda i: (0, i)),
-        compiler_params=pltpu.CompilerParams(vmem_limit_bytes=40 << 20),
-        cost_estimate=pl.CostEstimate(
-            flops=4 * tokens * width * groups * GROUP,
-            bytes_accessed=4 * width * groups * GROUP,
-            transcendentals=0,
-        ),
-    )(grads, codes, scales)
+            pl.BlockSpec(memory_space=pl.ANY),
+            pl.BlockSpec((GROUP, wide), lambda i: (jnp.minimum(i, groups - 1), 0)),
+            pl.BlockSpec((GROUP // 8, wide), lambda i: (jnp.minimum(i, groups - 1), 0)),
+        ],
+        out_specs=pl.BlockSpec((rows, span), lambda i: (0, jnp.maximum(i - DOWN_LAG, 0))),
+        scratch_shapes=[
+            pltpu.VMEM((n_col, here, wide), BF16),
+            pltpu.VMEM((groups, 2, chips, rows, span), BF16),
+            pltpu.VMEM((groups, chips, rows, span), BF16),
+            pltpu.VMEM((groups, chips, rows, span), BF16),
+            pltpu.VMEM((groups, chips - 1, rows, span), BF16),
+            dma,
+            dma((n_col - 1,)),
+            dma((n_col - 1,)),
+            dma((groups,)),
+            dma((groups,)),
+            dma((groups, chips - 1)),
+            dma((groups, chips - 1)),
+        ],
+        compiler_params=pltpu.CompilerParams(
+            collective_id=4, has_side_effects=True, vmem_limit_bytes=60 << 20,
+            dimension_semantics=("arbitrary",)),
+    )(out_grad, codes, scales)
 
 
 def act_kernel(hidden_units, ts_ref, hidden_ref, gate_ref, up_ref, out_ref):
@@ -336,9 +443,7 @@
     more = steps * SPAN - gate_scales.shape[1]
     gs = jnp.pad(half_scales(gate_scales), ((0, 0), (0, more)))
     us = jnp.pad(half_scales(up_scales), ((0, 0), (0, more)))
-    grads = lax.all_gather(out_grad, "col", axis=0, tiled=True)
-    partial = down(grads, down_codes, ds, groups)
-    hidden = lax.psum_scatter(partial, "row", scatter_dimension=0, tiled=True)
+    hidden = down(out_grad, down_codes.T, ds, groups, n_row, n_col)
     own = act(ts, hidden, gate_act, up_act, steps)
     unit, amax = width(ts, own, gate_codes, gs, up_codes, us, n_row, n_col)
     return unit, amax[0, 0:1]

time: 331 us -> 265 us (0.80)
  waiting for transfers between devices: 93.1 us -> 0 us
  Pallas kernels: 192 us -> 252 us
  local copies, waits for them, and re-layouts: 29.7 us -> 8.78 us
  between operations: 14.1 us -> 0.73 us
    reduce_scatter x1 -> x0, waiting for transfers between devices: 71.7 us -> none  [per_device(): hidden = lax.psum_scatter(partial, 'row', scatter_dimension=0, tiled=True)]
    pallas_call x1, Pallas kernels: 33.8 us -> 88.7 us  [down(): pl.pallas_call(functools.partial(down_kernel, n_row, n_col, groups), out_...]
    unnamed x22 -> x15, local copies, waits for them, and re-layouts: 26.4 us -> 4.53 us
    all_gather x1 -> x0, waiting for transfers between devices: 20.8 us -> none  [per_device(): grads = lax.all_gather(out_grad, 'col', axis=0, tiled=True)]
    pallas_call x1, Pallas kernels: 148 us -> 153 us  [width(): pl.pallas_call(functools.partial(width_kernel, n_row, n_col, steps), out_...]
  transfers between devices with their start and end apart: 2 -> 0, of which waited for: 2 -> 0; matrix products, arithmetic and copies ran while one was open for 6% -> 0% of each run, Pallas kernels for 0% -> 0%
where the time goes in v3:
time: 265 us; the launch traced here: 264 us
  Pallas kernels  252 us (95%)
  local copies, waits for them, and re-layouts  8.78 us (3%)
  other arithmetic  3.28 us (1%)
    pallas_call x1, Pallas kernels, width(): pl.pallas_call(functools.partial(width_kernel, n_row, n_col, steps), out_...  153 us
    pallas_call x1, Pallas kernels, down(): pl.pallas_call(functools.partial(down_kernel, n_row, n_col, groups), out_...  88.7 us
    pallas_call x1, Pallas kernels, act(): pl.pallas_call(functools.partial(act_kernel, gate_rows.shape[1]), out_sha...  9.82 us

profile of v3, /device:TPU:0, one launch (start us, length us, event | category | flops | bytes accessed | tf_op | source)
XLA Modules:
  0.0 264.5 jit_solution(17441167683496842031)
XLA Ops:
  0.6 2.1 multiply_convert_fusion.2
  2.7 1.0 pad.11.scale_ref
  3.8 0.0 copy-start.2
  3.8 0.0 copy-start.3
  3.8 0.0 copy-start.4
  3.8 88.7 %shard_map.113.hidden_ref = f32[80,7424]{1,0:T(8,128)} custom-call(bf16[160,1024]{1,0:T(8,128)(2,1)} %own_ref.1, s32[3696,1024]{1,0:T(8,128)} %bitcast.2, bf16[464,1024]{1,0:T(8,128)(2,1)} %pad.11.scale_ref), custom_call_target="tpu_custom_call" | custom-call | tf_op jit(solution)/shard_map/pallas_call | solution.py:170
  92.5 0.0 copy-done.2
  92.5 0.0 copy-done.3
  92.5 0.0 copy-done.4
  92.5 0.0 copy-start.1
  92.5 1.7 copy-done.1
  94.2 0.0 copy-start.5
  94.2 9.8 %shard_map.114.own_ref = bf16[15,2,80,512]{3,2,1,0:T(8,128)(2,1)S(1)} custom-call(f32[3]{0:T(128)S(1)} %copy-done.4, f32[80,7424]{1,0:T(8,128)S(1)} %copy-done.1, bf16[80,7392]{1,0:T(8,128)(2,1)S(1)} %copy-done.2, bf16[80,7392]{1,0:T(8,128)(2,1)S(1)} %copy-done.3), custom_call_target="tpu_custom_call" | custom-call | tf_op jit(solution)/shard_map/pallas_call | solution.py:226
  104.0 0.0 copy-done.5
  104.0 0.0 copy-start
  104.0 0.0 copy-start.6
  104.1 0.6 multiply_convert_fusion.1
  104.6 1.0 pad.12.gs_ref
  105.7 0.1 copy-done
  105.8 1.0 copy-done.6
  106.8 0.6 multiply_convert_fusion
  107.4 1.0 pad.13.us_ref
  108.4 153.1 %shard_map.115 = (bf16[160,1024]{1,0:T(8,128)(2,1)}, f32[8,128]{1,0:T(8,128)}) custom-call(f32[3]{0:T(128)} %ts_ref.3, bf16[15,2,80,512]{3,2,1,0:T(8,128)(2,1)} %copy-done, s32[7392,512]{1,0:T(8,128)} %gc_ref.1, bf16[64,7680]{1,0:T(8,128)(2,1)} %pad.12.gs_ref, s32[7392,512]{1,0:T(8,128)} %uc_ref.1, bf16[64,7680]{1,0:T(8,128)(2,1)} %pad.13.us_ref), custom_call_target="tpu_custom_call" | custom-call | tf_op jit(solution)/shard_map/pallas_call | solution.py:395
  261.6 1.2 slice.3
  262.8 1.7 copy.13
Async XLA Ops:
  3.8 88.7 %copy-start.2 = (bf16[80,7392]{1,0:T(8,128)(2,1)S(1)}, bf16[80,7392]{1,0:T(8,128)(2,1)}, u32[]{:S(2)}) copy-start(bf16[80,7392]{1,0:T(8,128)(2,1)} %gate_ref.1) | copy-start | bytes 3548164
  3.8 88.7 %copy-start.3 = (bf16[80,7392]{1,0:T(8,128)(2,1)S(1)}, bf16[80,7392]{1,0:T(8,128)(2,1)}, u32[]{:S(2)}) copy-start(bf16[80,7392]{1,0:T(8,128)(2,1)} %up_ref.1) | copy-start | bytes 3548164
  3.8 88.8 %copy-start.4 = (f32[3]{0:T(128)S(1)}, f32[3]{0:T(128)}, u32[]{:S(2)}) copy-start(f32[3]{0:T(128)} %ts_ref.3) | copy-start | bytes 40
  92.5 1.7 copy-start.1
  94.2 9.8 %copy-start.5 = (s32[64,7392]{1,0:T(8,128)S(1)}, s32[64,7392]{1,0:T(8,128)}, u32[]{:S(2)}) copy-start(s32[64,7392]{1,0:T(8,128)} %param.14) | copy-start | bytes 5677060
  104.0 1.8 copy-start
  104.0 2.8 %copy-start.6 = (s32[64,7392]{1,0:T(8,128)S(1)}, s32[64,7392]{1,0:T(8,128)}, u32[]{:S(2)}) copy-start(s32[64,7392]{1,0:T(8,128)} %param.16) | copy-start | bytes 5677060
